TPU v7x, 256 devices: a whole 4x4x8 slice. The times are simulated.
256 devices in a mesh: seq: 64 (over x, z, core), head: 4 (over y).
Axes of the slice: x: 4, y: 4, z: 8, core: 2. Of those that a mesh axis runs over, the one named last changes fastest.
Arguments:
- tree_queries: bfloat16 [4, 64, 128, 128], P(None, 'seq', 'head'), may hold values from -100 to 100
- tree_keys: bfloat16 [4, 64, 8, 128], P(None, 'seq', 'head'), may hold values from -12 to 12
- tree_values: bfloat16 [4, 64, 8, 128], P(None, 'seq', 'head'), may hold values from -6 to 6
- cache_keys: bfloat16 [4, 40960, 8, 128], P(None, 'seq', 'head'), may hold values from -6 to 6
- cache_values: bfloat16 [4, 40960, 8, 128], P(None, 'seq', 'head'), may hold values from -6 to 6
- out_weight: bfloat16 [16384, 16384], P('head', 'seq'), may hold values from -0.8984375 to 0.8984375
- context_lengths: int32 [4], replicated, may hold values from 5120 to 40952, as said below
- parents: int32 [4, 64], replicated, may hold values from -1 to 62, as said below
- accepted_nodes: int32 [4, 8], replicated, may hold values from 0 to 63, as said below
- accepted_count: int32 [4], replicated, may hold values from 1 to 8
Outputs:
- projected: bfloat16 [256, 16384], P('head', 'seq')
- keys_out: bfloat16 [4, 40960, 8, 128], P(None, 'seq', 'head')
- values_out: bfloat16 [4, 40960, 8, 128], P(None, 'seq', 'head')
Inputs may be any that keep to these rules, and one draw needn't show every extreme that they name: Request r's cache holds positions 0 to context_lengths[r] - 1; some request has the largest value in every draw. parents[r, 0] = -1 marks the root; for i >= 1, 0 <= parents[r, i] < i. `accepted_nodes`: each row lists distinct tree nodes in increasing order, the first being the root 0; entries j >= accepted_count[r] are not used.
All inputs are finite; a program needn't handle non-finite values.
Results may differ from a plain program's by a relative error of at most 0.0051.
Values may be sent and summed in bfloat16 or wider, within the bound.
No kernel may reach another device: no remote copies, remote signals or barrier semaphores. Data moves between devices by JAX's collectives and lax.ppermute only.
A program may use at most 64 MiB of HBM per device.

v0:
```python
import math
import jax
import jax.numpy as jnp
from jax import lax
from jax.sharding import PartitionSpec as P

NEG = -1e30


def passed_along(block, axis, distance):
    devices = range(lax.axis_size(axis))
    route = [((i - distance) % len(devices), i) for i in devices]
    return lax.ppermute(block, axis, route)


def ancestors(parents):
    count_nodes = parents.shape[1]
    columns = jnp.arange(count_nodes, dtype=jnp.int32)
    linked = (parents[:, :, None] == columns[None, None, :]) | (
        columns[:, None] == columns[None, :]
    )[None]
    closure = linked.astype(jnp.float32)
    for rounds in range(max(count_nodes - 1, 1).bit_length()):
        closure = jnp.minimum(jnp.matmul(closure, closure, precision=lax.Precision.HIGHEST), 1.0)
    return closure


def partial_attention(queries, keys, values, allowed, scale_factor):
    scores = (
        jnp.einsum("rnhge,rphe->rnhgp", queries, keys, preferred_element_type=jnp.float32)
        * scale_factor
    )
    row_top = jnp.max(jnp.where(allowed, scores, NEG), axis=-1)
    weights = jnp.where(allowed, jnp.exp(scores - row_top[..., None]), 0.0)
    row_sum = jnp.sum(weights, axis=-1)
    numerator = jnp.einsum(
        "rnhgp,rphe->rnhge",
        weights.astype(jnp.bfloat16),
        values,
        preferred_element_type=jnp.float32,
    )
    return (row_top, row_sum, numerator)


def merge_parts(first, second):
    top_first, sum_first, acc_first = first
    top_second, sum_second, acc_second = second
    row_top = jnp.maximum(top_first, top_second)
    scale_first = jnp.exp(top_first - row_top)
    scale_second = jnp.exp(top_second - row_top)
    row_sum = sum_first * scale_first + sum_second * scale_second
    numerator = acc_first * scale_first[..., None] + acc_second * scale_second[..., None]
    return (row_top, row_sum, numerator)


def append_rows(cache_block, tree_all, choose, slot_map, written):
    picked = jnp.einsum(
        "rjn,rnhe->rjhe", choose, tree_all, preferred_element_type=jnp.float32
    ).astype(jnp.bfloat16)
    placed = jnp.einsum(
        "rjp,rjhe->rphe", slot_map, picked, preferred_element_type=jnp.float32
    ).astype(jnp.bfloat16)
    return jnp.where(written[:, :, None, None], placed, cache_block)


def on_device(
    tree_queries,
    tree_keys,
    tree_values,
    cache_keys,
    cache_values,
    out_weight,
    context_lengths,
    parents,
    accepted_nodes,
    accepted_count,
):
    requests, ctx_local, kv_local, head_dim = cache_keys.shape
    node_local, q_local = (tree_queries.shape[1], tree_queries.shape[2])
    group_size = q_local // kv_local
    path_len = accepted_nodes.shape[1]
    scale_factor = 1.0 / math.sqrt(head_dim)
    seq_index = lax.axis_index("seq")
    seq_count = lax.axis_size("seq")
    nodes_all = node_local * seq_count
    offset = seq_index * ctx_local
    grouped = tree_queries.reshape(requests, node_local, kv_local, group_size, head_dim)
    tree_all_k, tree_all_v = (
        lax.all_gather(tree_keys, "seq", axis=1, tiled=True),
        lax.all_gather(tree_values, "seq", axis=1, tiled=True),
    )
    closure = ancestors(parents)
    home_rows = lax.dynamic_slice_in_dim(closure, seq_index * node_local, node_local, 1)
    tree_state = partial_attention(
        grouped, tree_all_k, tree_all_v, home_rows[:, :, None, None, :] > 0.5, scale_factor
    )
    positions = offset + jnp.arange(ctx_local, dtype=jnp.int32)
    usable = (positions[None, :] < context_lengths[:, None])[:, None, None, None, :]

    def turn(turn_number, carried):
        queries, row_top, row_sum, numerator = carried
        local_part = partial_attention(queries, cache_keys, cache_values, usable, scale_factor)
        row_top, row_sum, numerator = merge_parts((row_top, row_sum, numerator), local_part)
        queries = passed_along(queries, "seq", 1)
        row_top, row_sum, numerator = passed_along((row_top, row_sum, numerator), "seq", 1)
        return (queries, row_top, row_sum, numerator)

    start_top = jnp.full((requests, node_local, kv_local, group_size), NEG, jnp.float32)
    start_sum = jnp.zeros((requests, node_local, kv_local, group_size), jnp.float32)
    start_acc = jnp.zeros((requests, node_local, kv_local, group_size, head_dim), jnp.float32)
    finished = lax.fori_loop(0, seq_count, turn, (grouped, start_top, start_sum, start_acc))
    cache_state = (finished[1], finished[2], finished[3])
    final_top, final_sum, final_acc = merge_parts(cache_state, tree_state)
    attention = (
        (final_acc / final_sum[..., None])
        .astype(jnp.bfloat16)
        .reshape(requests, node_local, q_local * head_dim)
    )
    partial_terms = jnp.einsum(
        "rnx,xd->rnd",
        lax.all_gather(attention, "seq", axis=1, tiled=True),
        out_weight,
        preferred_element_type=jnp.float32,
    )
    partial_terms = partial_terms.reshape(requests * nodes_all, out_weight.shape[1])
    projected = lax.psum_scatter(partial_terms, "head", scatter_dimension=0, tiled=True).astype(
        jnp.bfloat16
    )
    choose = (
        accepted_nodes[:, :, None] == jnp.arange(nodes_all, dtype=jnp.int32)[None, None, :]
    ).astype(jnp.bfloat16)
    steps_index = jnp.arange(path_len, dtype=jnp.int32)
    targets = context_lengths[:, None] + steps_index[None, :] - offset
    alive = steps_index[None, :] < accepted_count[:, None]
    slot_flags = (
        targets[:, :, None] == jnp.arange(ctx_local, dtype=jnp.int32)[None, None, :]
    ) & alive[:, :, None]
    slot_map = slot_flags.astype(jnp.bfloat16)
    written = jnp.sum(slot_flags.astype(jnp.float32), axis=1) > 0.5
    keys_out = append_rows(cache_keys, tree_all_k, choose, slot_map, written)
    values_out = append_rows(cache_values, tree_all_v, choose, slot_map, written)
    return (projected, keys_out, values_out)


def solution(mesh):
    in_specs = (
        P(None, "seq", "head", None),
        P(None, "seq", "head", None),
        P(None, "seq", "head", None),
        P(None, "seq", "head", None),
        P(None, "seq", "head", None),
        P("head", "seq"),
        P(),
        P(),
        P(),
        P(),
    )
    out_specs = (P("head", "seq"), P(None, "seq", "head", None), P(None, "seq", "head", None))
    return jax.shard_map(
        on_device, mesh=mesh, in_specs=in_specs, out_specs=out_specs, check_vma=False
    )
```

profile of v0, /device:TPU:2, one launch (start us, length us, event | category | flops | bytes accessed | tf_op | source)
XLA Modules:
  0.0 925.1 jit_solution(13085080901726072045)
XLA Ops:
  10.5 56.6 %all_gather.9 = bf16[4,64,2,128]{3,0,2,1:T(4,128)(2,1)} all-gather(bf16[4,1,2,128]{3,0,2,1:T(4,128)(2,1)S(1)} %copy.33), channel_id=1, replica_groups=mesh['seq'=64,'head'=4] {'seq'}, dimensions={1}, use_global_device_ids=true | all-gather | bytes 133120 | tf_op jit(solution)/shard_map/all_gather | solution.py:89
  70.1 51.7 %all_gather.10 = bf16[4,64,2,128]{3,0,2,1:T(4,128)(2,1)} all-gather(bf16[4,1,2,128]{3,0,2,1:T(4,128)(2,1)S(1)} %copy.35), channel_id=1, replica_groups=mesh['seq'=64,'head'=4] {'seq'}, dimensions={1}, use_global_device_ids=true | all-gather | bytes 133120 | tf_op jit(solution)/shard_map/all_gather | solution.py:90
  122.9 645.8 %while.17 = (s32[]{:T(128)}, bf16[4,1,2,16,128]{4,3,2,0,1:T(8,128)(2,1)S(1)}, f32[4,1,2,16]{3,2,0,1:T(2,128)S(1)}, f32[4,1,2,16]{3,2,0,1:T(2,128)S(1)}, f32[4,1,...) while((s32[]{:T(128)}, ...), condition=%wide.region_3.4_spmd.clone, body=%wide.region_0.3_spmd.clone.sunk | while | flops 42732544 | bytes 9494321 | solution.py:111
  145.6 6.3 collective-permute-done.1
  155.2 6.3 collective-permute-done.1
  164.9 6.3 collective-permute-done.1
  174.5 6.3 collective-permute-done.1
  184.1 6.3 collective-permute-done.1
  193.7 6.3 collective-permute-done.1
  203.3 6.3 collective-permute-done.1
  213.0 6.3 collective-permute-done.1
  222.6 6.3 collective-permute-done.1
  232.2 6.3 collective-permute-done.1
  241.8 6.3 collective-permute-done.1
  251.5 6.3 collective-permute-done.1
  261.1 6.3 collective-permute-done.1
  270.7 6.3 collective-permute-done.1
  280.3 6.3 collective-permute-done.1
  289.9 6.3 collective-permute-done.1
  299.6 6.3 collective-permute-done.1
  309.2 6.3 collective-permute-done.1
  318.8 6.3 collective-permute-done.1
  328.4 6.3 collective-permute-done.1
  338.0 6.3 collective-permute-done.1
  347.7 6.3 collective-permute-done.1
  415.0 6.3 collective-permute-done.1
  424.6 6.3 collective-permute-done.1
  434.3 6.3 collective-permute-done.1
  443.9 6.3 collective-permute-done.1
  453.5 6.3 collective-permute-done.1
  771.1 118.9 %all-gather.2.cloned.1.call-done = bf16[4,64,4096]{2,0,1:T(4,128)(2,1)} async-done(((bf16[4,1,4096]{2,0,1:T(4,128)(2,1)}), bf16[4,64,4096]{2,0,1:T(4,128)(2,1)}) %all-gather.2.cloned.1.call-update) | async-done | bytes 2097168 | tf_op jit(solution)/shard_map/all_gather | solution.py:121
  906.2 10.7 %reduce-scatter.2.cloned.1.call-done = f32[64,256]{1,0:T(8,128)} async-done(((f32[256,256]{1,0:T(8,128)}), f32[64,256]{1,0:T(8,128)}) %reduce-scatter.2.cloned.1.call-update) | async-done | bytes 65552 | tf_op jit(solution)/shard_map/reduce_scatter | solution.py:126
  (1060 shorter events, 500.6 us)
Async XLA Ops:
  7.2 882.8 %all-gather.2.cloned.1.call-start = ((), (), s32[]{:S(2)}) async-start(), calls=%async_computation.1 | async-start | bytes 2129920 | tf_op jit(solution)/shard_map/all_gather | solution.py:121
  511.9 7.7 collective-permute-start.3
  522.8 7.7 collective-permute-start.3
  522.8 7.7 collective-permute-start
  533.6 7.7 collective-permute-start.3
  544.4 7.7 collective-permute-start.3
  555.2 7.7 collective-permute-start.3
  566.1 7.7 collective-permute-start.3
  566.1 7.7 collective-permute-start
  576.9 7.7 collective-permute-start.3
  587.7 7.7 collective-permute-start.3
  598.6 7.7 collective-permute-start.3
  609.4 7.7 collective-permute-start.3
  609.4 7.7 collective-permute-start
  620.2 7.7 collective-permute-start.3
  631.1 7.7 collective-permute-start.3
  641.9 7.7 collective-permute-start.3
  652.7 7.7 collective-permute-start.3
  652.7 7.7 collective-permute-start
  663.6 7.7 collective-permute-start.3
  674.4 7.7 collective-permute-start.3
  685.2 7.7 collective-permute-start.3
  685.2 7.7 collective-permute-start
  696.1 7.7 collective-permute-start.3
  696.1 7.7 collective-permute-start
  706.9 7.7 collective-permute-start.3
  717.7 7.7 collective-permute-start.3
  728.6 7.7 collective-permute-start.3
  739.4 7.7 collective-permute-start.3
  750.2 7.7 collective-permute-start.3
  761.1 7.7 collective-permute-start.3
  770.6 146.3 %reduce-scatter.2.cloned.1.call-start = ((), (), s32[]{:S(2)}) async-start(), calls=%async_computation.2 | async-start | bytes 327680 | tf_op jit(solution)/shard_map/reduce_scatter | solution.py:126
  (303 other events, 3517.4 us)
Sparse Core Ops, SparseCore 0:
  770.7 119.2 all-gather.1
  894.9 21.9 reduce-scatter.1
where the time goes:
time: 931 us; the launch traced here: 925 us
  waiting for transfers between devices  393 us (42%)
  starting transfers between devices  179 us (19%)
  matrix products  169 us (18%)
  blocking collectives  108 us (12%)
  local copies, waits for them, and re-layouts  36.9 us (4%)
  other arithmetic  22.3 us (2%)
  between operations  14.3 us (2%)
    ppermute x256, waiting for transfers between devices, passed_along(): return lax.ppermute(block, axis, route)  264 us
    ppermute x256, starting transfers between devices, passed_along(): return lax.ppermute(block, axis, route)  179 us
    dot_general x65, matrix products, partial_attention(): jnp.einsum('rnhgp,rphe->rnhge', weights.astype(jnp.bfloat16), values, pre...  119 us
    all_gather x1, waiting for transfers between devices, on_device(): lax.all_gather(attention, 'seq', axis=1, tiled=True)  119 us
    all_gather x1, blocking collectives, on_device(): lax.all_gather(tree_keys, 'seq', axis=1, tiled=True)  56.6 us
    all_gather x1, blocking collectives, on_device(): lax.all_gather(tree_values, 'seq', axis=1, tiled=True)  51.7 us
    dot_general x65, matrix products, partial_attention(): jnp.einsum('rnhge,rphe->rnhgp', queries, keys, preferred_element_type=jnp...  38.7 us
    while x192, local copies, waits for them, and re-layouts  24.2 us
  transfers between devices with their start and end apart: 258, of which 92 were waited for; matrix products, arithmetic and copies ran while one was open for 1% of the time, Pallas kernels for 0%

commit v1 on v0

--- a/solution.py
+++ b/solution.py
@@ -116,9 +116,17 @@
         .astype(jnp.bfloat16)
         .reshape(requests, node_local, q_local * head_dim)
     )
+
+    def fill_the_pieces_all(a0):
+        part_now = jax.lax.axis_size("seq")
+        row_out = jnp.stack(part_now * [a0])
+        tall = jax.lax.all_to_all(row_out, "seq", 0, 0)
+        after = jnp.concatenate(tall, axis=1)
+        return after
+
     partial_terms = jnp.einsum(
         "rnx,xd->rnd",
-        lax.all_gather(attention, "seq", axis=1, tiled=True),
+        fill_the_pieces_all(attention),
         out_weight,
         preferred_element_type=jnp.float32,
     )

time: 931 us -> 917 us (0.985)
  waiting for transfers between devices: 393 us -> 321 us
  starting transfers between devices: 179 us -> 236 us
    all_gather x1 -> x0, waiting for transfers between devices: 119 us -> none  [on_device(): lax.all_gather(attention, 'seq', axis=1, tiled=True)]
    all_to_all x0 -> x1, starting transfers between devices: none -> 54.4 us  [fill_the_pieces_all(): tall = jax.lax.all_to_all(row_out, 'seq', 0, 0)]
    all_to_all x0 -> x1, waiting for transfers between devices: none -> 48.7 us  [fill_the_pieces_all(): tall = jax.lax.all_to_all(row_out, 'seq', 0, 0)]
  transfers between devices with their start and end apart: 258 -> 258, of which waited for: 92 -> 93; matrix products, arithmetic and copies ran while one was open for 1% -> 1% of each run, Pallas kernels for 0% -> 0%
where the time goes in v1:
time: 917 us; the launch traced here: 911 us
  waiting for transfers between devices  321 us (35%)
  starting transfers between devices  236 us (26%)
  matrix products  166 us (18%)
  blocking collectives  108 us (12%)
  local copies, waits for them, and re-layouts  41.4 us (5%)
  other arithmetic  22.3 us (2%)
  between operations  14.3 us (2%)
    ppermute x256, waiting for transfers between devices, passed_along(): return lax.ppermute(block, axis, route)  261 us
    ppermute x256, starting transfers between devices, passed_along(): return lax.ppermute(block, axis, route)  181 us
    dot_general x65, matrix products, partial_attention(): jnp.einsum('rnhgp,rphe->rnhge', weights.astype(jnp.bfloat16), values, pre...  120 us
    all_gather x1, blocking collectives, on_device(): lax.all_gather(tree_keys, 'seq', axis=1, tiled=True)  56.3 us
    all_to_all x1, starting transfers between devices, fill_the_pieces_all(): tall = jax.lax.all_to_all(row_out, 'seq', 0, 0)  54.4 us
    all_gather x1, blocking collectives, on_device(): lax.all_gather(tree_values, 'seq', axis=1, tiled=True)  51.8 us
    all_to_all x1, waiting for transfers between devices, fill_the_pieces_all(): tall = jax.lax.all_to_all(row_out, 'seq', 0, 0)  48.7 us
    dot_general x65, matrix products, partial_attention(): jnp.einsum('rnhge,rphe->rnhgp', queries, keys, preferred_element_type=jnp...  38.7 us
  transfers between devices with their start and end apart: 258, of which 93 were waited for; matrix products, arithmetic and copies ran while one was open for 1% of the time, Pallas kernels for 0%

profile of v1, /device:TPU:2, one launch (start us, length us, event | category | flops | bytes accessed | tf_op | source)
XLA Modules:
  0.0 911.3 jit_solution(13071482364089437763)
XLA Ops:
  10.5 56.3 %all_gather.6 = bf16[4,64,2,128]{3,0,2,1:T(4,128)(2,1)} all-gather(bf16[4,1,2,128]{3,0,2,1:T(4,128)(2,1)S(1)} %copy.31), channel_id=1, replica_groups=mesh['seq'=64,'head'=4] {'seq'}, dimensions={1}, use_global_device_ids=true | all-gather | bytes 133120 | tf_op jit(solution)/shard_map/all_gather | solution.py:89
  69.8 51.8 %all_gather.7 = bf16[4,64,2,128]{3,0,2,1:T(4,128)(2,1)} all-gather(bf16[4,1,2,128]{3,0,2,1:T(4,128)(2,1)S(1)} %copy.33), channel_id=1, replica_groups=mesh['seq'=64,'head'=4] {'seq'}, dimensions={1}, use_global_device_ids=true | all-gather | bytes 133120 | tf_op jit(solution)/shard_map/all_gather | solution.py:90
  122.7 646.6 %while.17 = (s32[]{:T(128)}, bf16[4,1,2,16,128]{4,3,2,0,1:T(8,128)(2,1)S(1)}, f32[4,1,2,16]{3,2,0,1:T(2,128)S(1)}, f32[4,1,2,16]{3,2,0,1:T(2,128)S(1)}, f32[4,1,...) while((s32[]{:T(128)}, ...), condition=%wide.region_3.4_spmd.clone, body=%wide.region_0.3_spmd.clone.sunk | while | flops 42732544 | bytes 9494321 | solution.py:111
  145.3 6.3 collective-permute-done.1
  154.9 6.3 collective-permute-done.1
  164.6 6.3 collective-permute-done.1
  174.2 6.3 collective-permute-done.1
  183.8 6.3 collective-permute-done.1
  193.4 6.3 collective-permute-done.1
  203.1 6.3 collective-permute-done.1
  212.7 6.3 collective-permute-done.1
  222.3 6.3 collective-permute-done.1
  232.0 6.3 collective-permute-done.1
  241.6 6.3 collective-permute-done.1
  251.2 6.3 collective-permute-done.1
  260.8 6.3 collective-permute-done.1
  270.5 6.3 collective-permute-done.1
  280.1 6.3 collective-permute-done.1
  289.7 6.3 collective-permute-done.1
  299.4 6.3 collective-permute-done.1
  309.0 6.3 collective-permute-done.1
  318.6 6.3 collective-permute-done.1
  328.2 6.3 collective-permute-done.1
  347.5 6.3 collective-permute-done.1
  357.1 6.3 collective-permute-done.1
  376.4 6.3 collective-permute-done.1
  405.3 6.3 collective-permute-done.1
  424.5 6.3 collective-permute-done.1
  434.2 6.3 collective-permute-done.1
  772.8 54.4 %all-to-all-start = ((bf16[64,4,1,4096]{3,1,2,0:T(4,128)(2,1)}), bf16[64,4,1,4096]{3,1,2,0:T(4,128)(2,1)}, u32[]{:S(2)}, u32[]{:S(2)}) async-start(bf16[64,4,1,4096]{3,1,2,0:T(4,128)(2,1)} %stack.3), calls=%async_computation | async-start | bytes 4194304 | tf_op jit(solution)/shard_map/all_to_all | solution.py:123
  827.8 48.7 %all-to-all-done = bf16[64,4,1,4096]{3,1,2,0:T(4,128)(2,1)} async-done(((bf16[64,4,1,4096]{3,1,2,0:T(4,128)(2,1)}), bf16[64,4,1,4096]{3,1,2,0:T(4,128)(2,1)}, u32[]{:S(2)}, u32[]{:S(2)}) %all-to-all-start) | async-done | bytes 2097184 | tf_op jit(solution)/shard_map/all_to_all | solution.py:123
  892.2 10.8 %reduce-scatter.2.cloned.1.call-done = f32[64,256]{1,0:T(8,128)} async-done(((f32[256,256]{1,0:T(8,128)}), f32[64,256]{1,0:T(8,128)}) %reduce-scatter.2.cloned.1.call-update) | async-done | bytes 65552 | tf_op jit(solution)/shard_map/reduce_scatter | solution.py:134
  (1061 shorter events, 508.9 us)
Async XLA Ops:
  501.5 7.7 collective-permute-start.3
  501.5 7.7 collective-permute-start
  512.3 7.7 collective-permute-start.3
  523.2 7.7 collective-permute-start.3
  534.0 7.7 collective-permute-start.3
  534.0 7.7 collective-permute-start
  544.8 7.7 collective-permute-start.3
  555.7 7.7 collective-permute-start.3
  566.5 7.7 collective-permute-start.3
  577.4 7.7 collective-permute-start.3
  577.4 7.7 collective-permute-start
  588.2 7.7 collective-permute-start.3
  599.0 7.7 collective-permute-start.3
  609.9 7.7 collective-permute-start.3
  609.9 7.7 collective-permute-start
  620.7 7.7 collective-permute-start.3
  631.6 7.7 collective-permute-start.3
  642.4 7.7 collective-permute-start.3
  642.4 7.7 collective-permute-start
  653.2 7.7 collective-permute-start.3
  664.1 7.7 collective-permute-start.3
  674.9 7.7 collective-permute-start.3
  685.7 7.7 collective-permute-start.3
  696.6 7.7 collective-permute-start.3
  707.4 7.7 collective-permute-start.3
  718.3 7.7 collective-permute-start.3
  729.1 7.7 collective-permute-start.3
  739.9 7.7 collective-permute-start.3
  750.8 7.7 collective-permute-start.3
  761.6 7.7 collective-permute-start.3
  772.8 103.7 %all-to-all-start = ((bf16[64,4,1,4096]{3,1,2,0:T(4,128)(2,1)}), bf16[64,4,1,4096]{3,1,2,0:T(4,128)(2,1)}, u32[]{:S(2)}, u32[]{:S(2)}) async-start(bf16[64,4,1,4096]{3,1,2,0:T(4,128)(2,1)} %stack.3), calls=%async_computation | async-start | bytes 4194304 | tf_op jit(solution)/shard_map/all_to_all | solution.py:123
  827.3 75.7 %reduce-scatter.2.cloned.1.call-start = ((), (), s32[]{:S(2)}) async-start(), calls=%async_computation.2 | async-start | bytes 327680 | tf_op jit(solution)/shard_map/reduce_scatter | solution.py:134
  (303 other events, 2547.0 us)
Sparse Core Ops, SparseCore 0:
  880.9 22.0 reduce-scatter.1
